TPU v7x, 32 devices: a whole 2x2x4 slice. The times are simulated.
32 devices in a mesh: expert: 4 (over y, core), shard: 8 (over z, x).
Axes of the slice: x: 2, y: 2, z: 4, core: 2. Of those that a mesh axis runs over, the one named last changes fastest.
Arguments:
- tokens: bfloat16 [8192, 1536], P(('expert', 'shard')), may hold values from -6 to 6
- lengths: int32 [32], P(('expert', 'shard')), may hold values from 64 to 256, as said below
- routes: int32 [8192, 8], P(('expert', 'shard')), may hold values from 0 to 19, all different within a row; in each aligned block of 256 rows (0 to 255, 256 to 511, ...) at most 104 rows name the same one
- cotangent: bfloat16 [8192, 1536], P(('expert', 'shard')), may hold values from -6 to 6
- first_gain: bfloat16 [1536], P('shard'), may hold values from 0.5 to 1.5
- query_weight: bfloat16 [1536, 1536], P('shard'), may hold values from -0.15625 to 0.15625
- key_matrix: bfloat16 [1536, 512], P('shard'), may hold values from -0.15625 to 0.15625
- value_matrix: bfloat16 [1536, 512], P('shard'), may hold values from -0.15625 to 0.15625
- output_weight: bfloat16 [1536, 1536], P('shard'), may hold values from -1.25 to 1.25
- second_gain: bfloat16 [1536], P('shard'), may hold values from 0.5 to 1.5
- router_weight: bfloat16 [1536, 20], P('shard'), may hold values from -0.078125 to 0.078125
- gate_up_weight: bfloat16 [1536, 20, 1024], P('shard', 'expert'), may hold values from -0.15625 to 0.15625
- down_weight: bfloat16 [1536, 20, 512], P('shard', 'expert'), may hold values from -1 to 1
Outputs:
- layer_out: bfloat16 [8192, 1536], P(('expert', 'shard'))
- tokens_grad: float32 [8192, 1536], P(('expert', 'shard'))
- first_gain_grad: float32 [1536], P('shard')
- query_grad: float32 [1536, 1536], P('shard')
- key_grad: float32 [1536, 512], P('shard')
- value_grad: float32 [1536, 512], P('shard')
- output_grad: float32 [1536, 1536], P('shard')
- second_gain_grad: float32 [1536], P('shard')
- router_grad: float32 [1536, 20], P('shard')
- gate_up_grad: float32 [1536, 20, 1024], P('shard', 'expert')
- down_grad: float32 [1536, 20, 512], P('shard', 'expert')
Inputs may be any that keep to these rules, and one draw needn't show every extreme that they name: `lengths`: some sequence has 256 valid tokens and some 256 // 4. `routes`: each row names 8 different experts; among the 256 rows of one sequence no expert is named more than 104 times, a bound that some block reaches.
All inputs are finite; a program needn't handle non-finite values.
Results may differ from a plain program's by a relative error of at most 0.02.
Values may be sent and summed in bfloat16 or wider, within the bound.
A program may use at most 320 MiB of HBM per device.

v0:
```python
import jax
import jax.numpy as jnp
from jax import lax
from jax.sharding import PartitionSpec as P

HEAD_DIM = 64
norm_eps = 1e-06


def product(form, left, right):
    return jnp.einsum(form, left, right, preferred_element_type=jnp.float32)


def rope_tables(row_count, head_width):
    half_width = head_width // 2
    frequency = 10000.0 ** (-(jnp.arange(half_width, dtype=jnp.float32) * (2.0 / head_width)))
    angles = jnp.arange(row_count, dtype=jnp.float32)[:, None] * frequency[None, :]
    return (jnp.cos(angles)[:, None, :], jnp.sin(angles)[:, None, :])


def rotate(values_in, cosine, sine_table):
    half_width = values_in.shape[-1] // 2
    first_half = values_in[..., :half_width]
    second_half = values_in[..., half_width:]
    return jnp.concatenate(
        [
            first_half * cosine - second_half * sine_table,
            second_half * cosine + first_half * sine_table,
        ],
        axis=-1,
    )


def unrotate(grad_in, cosine, sine_table):
    half_width = grad_in.shape[-1] // 2
    first_half = grad_in[..., :half_width]
    second_half = grad_in[..., half_width:]
    return jnp.concatenate(
        [
            first_half * cosine + second_half * sine_table,
            second_half * cosine - first_half * sine_table,
        ],
        axis=-1,
    )


def norm_back(upstream, source, inv_scale, gain_vec):
    scaled = upstream * gain_vec
    gain_grad = jnp.sum(upstream * source * inv_scale, axis=0)
    grad_out = inv_scale * (
        scaled - source * inv_scale * inv_scale * jnp.mean(scaled * source, axis=-1, keepdims=True)
    )
    return (grad_out, gain_grad)


def on_device(
    tokens,
    lengths,
    routes,
    cotangent,
    first_gain,
    query_weight,
    key_matrix,
    value_matrix,
    output_weight,
    second_gain,
    router_weight,
    gate_up_weight,
    down_weight,
):
    seq_len, model_width = tokens.shape
    route_width = routes.shape[1]
    q_heads = query_weight.shape[1] // HEAD_DIM
    kv_heads = key_matrix.shape[1] // HEAD_DIM
    group_size = q_heads // kv_heads
    experts_all = router_weight.shape[1]
    local_experts = gate_up_weight.shape[1]
    inner_width = down_weight.shape[2]
    owners = lax.axis_size("expert")
    slot_count = 8 * max(
        seq_len // 32, (seq_len * route_width + 8 * experts_all - 1) // (8 * experts_all)
    )
    score_factor = HEAD_DIM ** (-0.5)
    gain_one, query_full, key_complete, value_complete, output_full, gain_two, router_full = (
        lax.all_gather(first_gain, "shard", axis=0, tiled=True),
        lax.all_gather(query_weight, "shard", axis=0, tiled=True),
        lax.all_gather(key_matrix, "shard", axis=0, tiled=True),
        lax.all_gather(value_matrix, "shard", axis=0, tiled=True),
        lax.all_gather(output_weight, "shard", axis=0, tiled=True),
        lax.all_gather(second_gain, "shard", axis=0, tiled=True),
        lax.all_gather(router_weight, "shard", axis=0, tiled=True),
    )
    gate_up_full, down_full = (
        lax.all_gather(gate_up_weight, "shard", axis=0, tiled=True),
        lax.all_gather(down_weight, "shard", axis=0, tiled=True),
    )
    gain_one = gain_one.astype(jnp.float32)
    gain_two = gain_two.astype(jnp.float32)
    cosine, sine_table = rope_tables(seq_len, HEAD_DIM)
    source = tokens.astype(jnp.float32)
    first_scale = lax.rsqrt(jnp.mean(source * source, axis=-1, keepdims=True) + norm_eps)
    first_norm_output = (source * first_scale * gain_one).astype(jnp.bfloat16)
    queries = rotate(
        product("za,ao->zo", first_norm_output, query_full).reshape(seq_len, q_heads, HEAD_DIM),
        cosine,
        sine_table,
    )
    queries = queries.astype(jnp.bfloat16).reshape(seq_len, kv_heads, group_size, HEAD_DIM)
    key_row_block = rotate(
        product("za,ao->zo", first_norm_output, key_complete).reshape(seq_len, kv_heads, HEAD_DIM),
        cosine,
        sine_table,
    ).astype(jnp.bfloat16)
    value_row_block = (
        product("za,ao->zo", first_norm_output, value_complete)
        .astype(jnp.bfloat16)
        .reshape(seq_len, kv_heads, HEAD_DIM)
    )
    position = jnp.arange(seq_len, dtype=jnp.int32)
    length = lengths[0]
    allowed = (position[None, :] <= position[:, None]) & (position[None, :] < length)
    scores = jnp.where(
        allowed, product("qhgd,khd->hgqk", queries, key_row_block) * score_factor, -1e30
    )
    row_max = jnp.max(scores, axis=-1, keepdims=True)
    shifted = jnp.exp(scores - row_max)
    row_total = jnp.sum(shifted, axis=-1, keepdims=True)
    log_total = row_max + jnp.log(row_total)
    probs_low = (shifted / row_total).astype(jnp.bfloat16)
    mixed_heads = (
        product("hgqk,khd->qhgd", probs_low, value_row_block)
        .reshape(seq_len, q_heads * HEAD_DIM)
        .astype(jnp.bfloat16)
    )
    hidden = source + product("sf,df->sd", mixed_heads, output_full)
    second_scale = lax.rsqrt(jnp.mean(hidden * hidden, axis=-1, keepdims=True) + norm_eps)
    second_normed = (hidden * second_scale * gain_two).astype(jnp.bfloat16)
    logits = product("sd,de->se", second_normed, router_full)
    chosen = (routes[:, :, None] == jnp.arange(experts_all, dtype=jnp.int32)).astype(jnp.float32)
    picked = jnp.sum(chosen * logits[:, None, :], axis=-1)
    gate_soft = jax.nn.softmax(picked, axis=-1)
    valid_rows = (position < length).astype(jnp.float32)
    routed = jnp.sum(chosen, axis=1) * valid_rows[:, None]
    earlier = (position[None, :] < position[:, None]).astype(jnp.bfloat16)
    rank_rows = product("st,te->se", earlier, routed.astype(jnp.bfloat16))
    slot_ids = jnp.arange(slot_count, dtype=jnp.float32)
    placing = (routed.T[:, None, :] * (rank_rows.T[:, None, :] == slot_ids[None, :, None])).astype(
        jnp.bfloat16
    )
    outgoing = (
        product("ems,sd->emd", placing, second_normed)
        .astype(jnp.bfloat16)
        .reshape(owners, local_experts, slot_count, model_width)
    )
    row_block = lax.all_to_all(outgoing, "expert", split_axis=0, concat_axis=0, tiled=True)
    both_pre = product("oemd,def->oemf", row_block, gate_up_full)
    active = (jax.nn.silu(both_pre[..., :inner_width]) * both_pre[..., inner_width:]).astype(
        jnp.bfloat16
    )
    answer = product("oemf,def->oemd", active, down_full).astype(jnp.bfloat16)
    returned = lax.all_to_all(answer, "expert", split_axis=0, concat_axis=0, tiled=True).reshape(
        experts_all, slot_count, model_width
    )
    gate_full = product("ske,sk->se", chosen.astype(jnp.bfloat16), gate_soft.astype(jnp.bfloat16))
    placing_float = placing.astype(jnp.float32)
    combine = (placing_float * gate_full.T[:, None, :]).astype(jnp.bfloat16)
    output = (hidden + product("ems,emd->sd", combine, returned)).astype(jnp.bfloat16)
    dout_full = cotangent.astype(jnp.float32) * valid_rows[:, None]
    dout_low = dout_full.astype(jnp.bfloat16)
    grad_rows = (
        product("ems,sd->emd", combine, dout_low)
        .astype(jnp.bfloat16)
        .reshape(owners, local_experts, slot_count, model_width)
    )
    incoming = lax.all_to_all(grad_rows, "expert", split_axis=0, concat_axis=0, tiled=True)
    answer_dot = product("emd,sd->ems", returned, dout_low)
    gate_grad_full = jnp.sum(placing_float * answer_dot, axis=1)
    gate_grad = jnp.sum(chosen * gate_grad_full.T[:, None, :], axis=-1)
    inner_sum = jnp.sum(gate_soft * gate_grad, axis=-1, keepdims=True)
    picked_grad = gate_soft * (gate_grad - inner_sum)
    logits_grad = jnp.sum(chosen * picked_grad[:, :, None], axis=1).astype(jnp.bfloat16)
    router_term = product("sd,se->de", second_normed, logits_grad)
    gate_up_full, down_full = (
        lax.all_gather(gate_up_weight, "shard", axis=0, tiled=True),
        lax.all_gather(down_weight, "shard", axis=0, tiled=True),
    )
    gate_part = both_pre[..., :inner_width]
    up_part = both_pre[..., inner_width:]
    sigmoid_gate = jax.nn.sigmoid(gate_part)
    silu_gate = gate_part * sigmoid_gate
    active_again = (silu_gate * up_part).astype(jnp.bfloat16)
    active_grad = product("oemd,def->oemf", incoming, down_full)
    both_grad = jnp.concatenate(
        [
            active_grad * up_part * sigmoid_gate * (1.0 + gate_part * (1.0 - sigmoid_gate)),
            active_grad * silu_gate,
        ],
        axis=-1,
    ).astype(jnp.bfloat16)
    row_grad = product("oemf,def->oemd", both_grad, gate_up_full).astype(jnp.bfloat16)
    gate_up_term = product("oemd,oemf->def", row_block, both_grad)
    down_term = product("oemd,oemf->def", incoming, active_again)
    back_rows = lax.all_to_all(row_grad, "expert", split_axis=0, concat_axis=0, tiled=True).reshape(
        experts_all, slot_count, model_width
    )
    gate_up_total, down_total = (
        lax.psum_scatter(
            gate_up_term.astype(jnp.bfloat16), "shard", scatter_dimension=0, tiled=True
        ).astype(jnp.float32),
        lax.psum_scatter(
            down_term.astype(jnp.bfloat16), "shard", scatter_dimension=0, tiled=True
        ).astype(jnp.float32),
    )
    normed_grad = product("ems,emd->sd", placing, back_rows) + product(
        "se,de->sd", logits_grad, router_full
    )
    hidden_grad, second_gain_term = norm_back(normed_grad, hidden, second_scale, gain_two)
    hidden_grad = hidden_grad + dout_full
    attn_grad = hidden_grad.astype(jnp.bfloat16)
    output_term = product("sd,sf->df", attn_grad, mixed_heads)
    mixed_grad = (
        product("za,ao->zo", attn_grad, output_full)
        .astype(jnp.bfloat16)
        .reshape(seq_len, kv_heads, group_size, HEAD_DIM)
    )
    scores_again = jnp.where(
        allowed, product("qhgd,khd->hgqk", queries, key_row_block) * score_factor, -1e30
    )
    probs_again = jnp.exp(scores_again - log_total)
    probs_grad = product("qhgd,khd->hgqk", mixed_grad, value_row_block)
    row_inner = jnp.sum(probs_again * probs_grad, axis=-1, keepdims=True)
    scores_grad = (probs_again * (probs_grad - row_inner)).astype(jnp.bfloat16)
    query_back = product("hgqk,khd->qhgd", scores_grad, key_row_block) * score_factor
    key_back = product("hgqk,qhgd->khd", scores_grad, queries) * score_factor
    value_back = product("hgqk,qhgd->khd", probs_again.astype(jnp.bfloat16), mixed_grad)
    query_pre = (
        unrotate(query_back.reshape(seq_len, q_heads, HEAD_DIM), cosine, sine_table)
        .astype(jnp.bfloat16)
        .reshape(seq_len, q_heads * HEAD_DIM)
    )
    key_pre = (
        unrotate(key_back, cosine, sine_table)
        .astype(jnp.bfloat16)
        .reshape(seq_len, kv_heads * HEAD_DIM)
    )
    value_pre = value_back.astype(jnp.bfloat16).reshape(seq_len, kv_heads * HEAD_DIM)
    query_term = product("sd,sf->df", first_norm_output, query_pre)
    key_term = product("sd,sf->df", first_norm_output, key_pre)
    value_term = product("sd,sf->df", first_norm_output, value_pre)
    normed1_grad = (
        product("sf,df->sd", query_pre, query_full)
        + product("sf,df->sd", key_pre, key_complete)
        + product("sf,df->sd", value_pre, value_complete)
    )
    tokens_grad, first_gain_term = norm_back(normed1_grad, source, first_scale, gain_one)
    tokens_grad = tokens_grad + hidden_grad
    mixer_sums = (
        lax.psum_scatter(
            first_gain_term.astype(jnp.bfloat16), "shard", scatter_dimension=0, tiled=True
        ).astype(jnp.float32),
        lax.psum_scatter(
            query_term.astype(jnp.bfloat16), "shard", scatter_dimension=0, tiled=True
        ).astype(jnp.float32),
        lax.psum_scatter(
            key_term.astype(jnp.bfloat16), "shard", scatter_dimension=0, tiled=True
        ).astype(jnp.float32),
        lax.psum_scatter(
            value_term.astype(jnp.bfloat16), "shard", scatter_dimension=0, tiled=True
        ).astype(jnp.float32),
        lax.psum_scatter(
            output_term.astype(jnp.bfloat16), "shard", scatter_dimension=0, tiled=True
        ).astype(jnp.float32),
        lax.psum_scatter(
            second_gain_term.astype(jnp.bfloat16), "shard", scatter_dimension=0, tiled=True
        ).astype(jnp.float32),
        lax.psum_scatter(
            router_term.astype(jnp.bfloat16), "shard", scatter_dimension=0, tiled=True
        ).astype(jnp.float32),
    )
    mixer_sums = (
        lax.psum(mixer_sums[0].astype(jnp.bfloat16), "expert").astype(jnp.float32),
        lax.psum(mixer_sums[1].astype(jnp.bfloat16), "expert").astype(jnp.float32),
        lax.psum(mixer_sums[2].astype(jnp.bfloat16), "expert").astype(jnp.float32),
        lax.psum(mixer_sums[3].astype(jnp.bfloat16), "expert").astype(jnp.float32),
        lax.psum(mixer_sums[4].astype(jnp.bfloat16), "expert").astype(jnp.float32),
        lax.psum(mixer_sums[5].astype(jnp.bfloat16), "expert").astype(jnp.float32),
        lax.psum(mixer_sums[6].astype(jnp.bfloat16), "expert").astype(jnp.float32),
    )
    return (
        output,
        tokens_grad,
        mixer_sums[0],
        mixer_sums[1],
        mixer_sums[2],
        mixer_sums[3],
        mixer_sums[4],
        mixer_sums[5],
        mixer_sums[6],
        gate_up_total,
        down_total,
    )


def solution(mesh):
    placed = (
        P(("expert", "shard"), None),
        P(("expert", "shard")),
        P(("expert", "shard"), None),
        P(("expert", "shard"), None),
        P("shard"),
        P("shard", None),
        P("shard", None),
        P("shard", None),
        P("shard", None),
        P("shard"),
        P("shard", None),
        P("shard", "expert", None),
        P("shard", "expert", None),
    )
    return jax.shard_map(
        on_device,
        mesh=mesh,
        in_specs=placed,
        out_specs=(
            P(("expert", "shard"), None),
            P(("expert", "shard"), None),
            P("shard"),
            P("shard", None),
            P("shard", None),
            P("shard", None),
            P("shard", None),
            P("shard"),
            P("shard", None),
            P("shard", "expert", None),
            P("shard", "expert", None),
        ),
        check_vma=False,
    )
```

profile of v0, /device:TPU:0, one launch (start us, length us, event | category | flops | bytes accessed | tf_op | source)
XLA Modules:
  0.0 1752.7 jit_solution(12676118598216443781)
XLA Ops:
  13.8 23.5 %all-reduce.5 = (bf16[1536]{0:T(1024)(128)(2,1)S(1)}, bf16[1536]{0:T(1024)(128)(2,1)S(1)}) all-reduce(bf16[1536]{0:T(1024)(128)(2,1)S(1)} %dynamic-update-slice, bf16[1536]{0:T(1024)(128)(2,1)S(1)} %dynamic-update-slice.1), channel_id=1, replica_groups=mesh['expert'=4,'shard'=8] {'shard'}, use_global_device_ids=true, to_apply=%add | all-reduce | flops 3072 | bytes 12288
  38.1 19.4 %all-gather.8.cloned.1.call-done = bf16[1536,512]{1,0:T(8,128)(2,1)} async-done(((bf16[192,512]{1,0:T(8,128)(2,1)}), bf16[1536,512]{1,0:T(8,128)(2,1)}) %all-gather.8.cloned.1.call-update) | async-done | bytes 1572880 | tf_op jit(solution)/shard_map/all_gather | solution.py:88
  59.7 42.6 %all-gather.10.cloned.1.call-done = bf16[1536,512]{1,0:T(8,128)(2,1)} async-done(((bf16[192,512]{1,0:T(8,128)(2,1)}), bf16[1536,512]{1,0:T(8,128)(2,1)}) %all-gather.10.cloned.1.call-update) | async-done | bytes 1572880 | tf_op jit(solution)/shard_map/all_gather | solution.py:87
  104.6 77.6 %all-gather.12.cloned.1.call-done = bf16[1536,1536]{1,0:T(8,128)(2,1)} async-done(((bf16[192,1536]{1,0:T(8,128)(2,1)}), bf16[1536,1536]{1,0:T(8,128)(2,1)}) %all-gather.12.cloned.1.call-update) | async-done | bytes 4718608 | tf_op jit(solution)/shard_map/all_gather | solution.py:86
  191.8 70.1 %all-gather.14.cloned.1.call-done = bf16[1536,1536]{1,0:T(8,128)(2,1)} async-done(((bf16[192,1536]{1,0:T(8,128)(2,1)}), bf16[1536,1536]{1,0:T(8,128)(2,1)}) %all-gather.14.cloned.1.call-update) | async-done | bytes 4718608 | tf_op jit(solution)/shard_map/all_gather | solution.py:89
  267.9 75.5 %all_to_all.20 = bf16[4,5,104,1536]{3,2,1,0:T(8,128)(2,1)} all-to-all(bf16[4,5,104,1536]{3,2,1,0:T(8,128)(2,1)S(1)} %bitcast.174), channel_id=1, replica_groups=mesh['expert'=4,'shard'=8] {'expert'}, dimensions={0} | all-to-all | bytes 12779520 | tf_op jit(solution)/shard_map/all_to_all | solution.py:155
  343.4 133.5 %all-gather.16.cloned.1.call-done = bf16[1536,5,1024]{2,0,1:T(8,128)(2,1)} async-done(((bf16[192,5,1024]{2,0,1:T(8,128)(2,1)}), bf16[1536,5,1024]{2,0,1:T(8,128)(2,1)}) %all-gather.16.cloned.1.call-update) | async-done | bytes 15728656 | tf_op jit(solution)/shard_map/all_gather | solution.py:94
  476.9 12.1 fusion.26
  495.2 99.9 %all-gather.18.cloned.1.call-done = bf16[1536,5,512]{2,0,1:T(8,128)(2,1)} async-done(((bf16[192,5,512]{2,0,1:T(8,128)(2,1)}), bf16[1536,5,512]{2,0,1:T(8,128)(2,1)}) %all-gather.18.cloned.1.call-update) | async-done | bytes 7864336 | tf_op jit(solution)/shard_map/all_gather | solution.py:95
  616.5 30.6 %all-gather = bf16[8,192,20]{1,2,0:T(8,128)(2,1)S(1)} all-gather(bf16[1,192,20]{1,2,0:T(8,128)(2,1)S(1)} %bitcast.202), channel_id=1, replica_groups=mesh['expert'=4,'shard'=8] {'shard'}, dimensions={0}, use_global_device_ids=true | all-gather | bytes 69120 | tf_op jit(solution)/shard_map/all_gather | solution.py:91
  647.5 40.7 %all-to-all-done.1 = bf16[4,5,104,1536]{3,2,1,0:T(8,128)(2,1)} async-done(((bf16[4,5,104,1536]{3,2,1,0:T(8,128)(2,1)}), bf16[4,5,104,1536]{3,2,1,0:T(8,128)(2,1)}, u32[]{:S(2)}, u32[]{:S(2)}) %all-to-all-start.1) | async-done | bytes 6389792 | tf_op jit(solution)/shard_map/all_to_all | solution.py:161
  696.6 75.7 %all_to_all.21 = bf16[4,5,104,1536]{3,2,1,0:T(8,128)(2,1)} all-to-all(bf16[4,5,104,1536]{3,2,1,0:T(8,128)(2,1)S(1)} %bitcast.180), channel_id=1, replica_groups=mesh['expert'=4,'shard'=8] {'expert'}, dimensions={0} | all-to-all | bytes 12779520 | tf_op jit(solution)/shard_map/all_to_all | solution.py:175
  772.3 14.0 fusion.23
  786.2 13.4 convert_bitcast_fusion
  811.1 71.5 %all-to-all-done.3 = bf16[4,5,104,1536]{3,2,1,0:T(8,128)(2,1)} async-done(((bf16[4,5,104,1536]{3,2,1,0:T(8,128)(2,1)}), bf16[4,5,104,1536]{3,2,1,0:T(8,128)(2,1)}, u32[]{:S(2)}, u32[]{:S(2)}) %all-to-all-start.3) | async-done | bytes 6389792 | tf_op jit(solution)/shard_map/all_to_all | solution.py:203
  931.9 34.8 %reduce-scatter.18.cloned.1.call-done = bf16[192,512]{1,0:T(8,128)(2,1)} async-done(((bf16[1536,512]{1,0:T(8,128)(2,1)}), bf16[192,512]{1,0:T(8,128)(2,1)}) %reduce-scatter.18.cloned.1.call-update) | async-done | bytes 196624 | tf_op jit(solution)/shard_map/reduce_scatter | solution.py:267
  966.7 68.2 %reduce-scatter.16.cloned.1.call-done = bf16[192,512]{1,0:T(8,128)(2,1)} async-done(((bf16[1536,512]{1,0:T(8,128)(2,1)}), bf16[192,512]{1,0:T(8,128)(2,1)}) %reduce-scatter.16.cloned.1.call-update) | async-done | bytes 196624 | tf_op jit(solution)/shard_map/reduce_scatter | solution.py:264
  1034.9 98.3 %reduce-scatter.20.cloned.1.call-done = bf16[192,1536]{1,0:T(8,128)(2,1)} async-done(((bf16[1536,1536]{1,0:T(8,128)(2,1)}), bf16[192,1536]{1,0:T(8,128)(2,1)}) %reduce-scatter.20.cloned.1.call-update) | async-done | bytes 589840 | tf_op jit(solution)/shard_map/reduce_scatter | solution.py:270
  1133.2 98.8 %reduce-scatter.14.cloned.1.call-done = bf16[192,1536]{1,0:T(8,128)(2,1)} async-done(((bf16[1536,1536]{1,0:T(8,128)(2,1)}), bf16[192,1536]{1,0:T(8,128)(2,1)}) %reduce-scatter.14.cloned.1.call-update) | async-done | bytes 589840 | tf_op jit(solution)/shard_map/reduce_scatter | solution.py:261
  1253.9 15.1 bitcast_convert_fusion
  1269.0 20.8 %copy.124 = bf16[1536,5120]{1,0:T(8,128)(2,1)} copy(bf16[1536,5120]{0,1:T(8,128)(2,1)} %bitcast.175) | data formatting | bytes 31457280
  1306.1 19.7 %all-reduce.4 = (bf16[1536]{0:T(1024)(128)(2,1)S(1)}, bf16[1536]{0:T(1024)(128)(2,1)S(1)}) all-reduce(bf16[1536]{0:T(1024)(128)(2,1)S(1)} %get-tuple-element.57, bf16[1536]{0:T(1024)(128)(2,1)S(1)} %copy-done.32), channel_id=2, replica_groups=mesh['expert'=4,'shard'=8] {'shard'}, use_global_device_ids=true, to_apply=%region_16.17.clone | all-reduce | flops 3072 | bytes 12288
  1349.3 136.9 %reduce-scatter.26.cloned.1.call-done = bf16[192,2560]{1,0:T(8,128)(2,1)} async-done(((bf16[1536,2560]{1,0:T(8,128)(2,1)}), bf16[192,2560]{1,0:T(8,128)(2,1)}) %reduce-scatter.26.cloned.1.call-update) | async-done | bytes 983056
  1489.4 250.7 %reduce-scatter.24.cloned.1.call-done = bf16[192,5120]{1,0:T(8,128)(2,1)} async-done(((bf16[1536,5120]{1,0:T(8,128)(2,1)}), bf16[192,5120]{1,0:T(8,128)(2,1)}) %reduce-scatter.24.cloned.1.call-update) | async-done | bytes 1966096
  (204 shorter events, 192.2 us)
Async XLA Ops:
  7.2 50.3 %all-gather.8.cloned.1.call-start = ((), (), s32[]{:S(2)}) async-start(), calls=%async_computation.11 | async-start | bytes 1769472 | tf_op jit(solution)/shard_map/all_gather | solution.py:88
  7.9 94.4 %all-gather.10.cloned.1.call-start = ((), (), s32[]{:S(2)}) async-start(), calls=%async_computation.12 | async-start | bytes 1769472 | tf_op jit(solution)/shard_map/all_gather | solution.py:87
  8.7 173.5 %all-gather.12.cloned.1.call-start = ((), (), s32[]{:S(2)}) async-start(), calls=%async_computation.13 | async-start | bytes 5308416 | tf_op jit(solution)/shard_map/all_gather | solution.py:86
  9.4 252.5 %all-gather.14.cloned.1.call-start = ((), (), s32[]{:S(2)}) async-start(), calls=%async_computation.14 | async-start | bytes 5308416 | tf_op jit(solution)/shard_map/all_gather | solution.py:89
  10.0 466.8 %all-gather.16.cloned.1.call-start = ((), (), s32[]{:S(2)}) async-start(), calls=%async_computation.15 | async-start | bytes 17694720 | tf_op jit(solution)/shard_map/all_gather | solution.py:94
  10.6 584.4 %all-gather.18.cloned.1.call-start = ((), (), s32[]{:S(2)}) async-start(), calls=%async_computation.16 | async-start | bytes 8847360 | tf_op jit(solution)/shard_map/all_gather | solution.py:95
  11.9 676.4 %copy-start.36 = (f32[256]{0:T(256)}, f32[256]{0:T(256)S(1)}, u32[]{:S(2)}) copy-start(f32[256]{0:T(256)S(1)} %fusion.100) | copy-start | bytes 3076
  37.6 887.8 %copy-start.24 = (f32[256]{0:T(256)}, f32[256]{0:T(256)S(1)}, u32[]{:S(2)}) copy-start(f32[256]{0:T(256)S(1)} %add_rsqrt_fusion.1) | copy-start | bytes 3076
  37.6 845.0 %copy-start.26 = (bf16[20,256]{1,0:T(8,128)(2,1)}, bf16[20,256]{1,0:T(8,128)(2,1)S(1)}, u32[]{:S(2)}) copy-start(bf16[20,256]{1,0:T(8,128)(2,1)S(1)} %multiply_bitcast_fusion) | copy-start | bytes 30724
  37.8 844.8 %copy-start.28 = (f32[20,256]{1,0:T(8,128)}, f32[20,256]{1,0:T(8,128)S(1)}, u32[]{:S(2)}) copy-start(f32[20,256]{1,0:T(8,128)S(1)} %fusion.83) | copy-start | bytes 61444
  59.7 129.4 %copy-start.15 = (bf16[256,512]{0,1:T(8,128)(2,1)}, bf16[256,512]{0,1:T(8,128)(2,1)S(1)}, u32[]{:S(2)}) copy-start(bf16[256,512]{0,1:T(8,128)(2,1)S(1)} %copy.83) | copy-start | bytes 786436
  104.6 82.2 %copy-start.19 = (bf16[256,8,32]{0,2,1:T(8,128)(2,1)}, bf16[256,8,32]{0,2,1:T(8,128)(2,1)S(1)}, u32[]{:S(2)}) copy-start(bf16[256,8,32]{0,2,1:T(8,128)(2,1)S(1)} %get-tuple-element.82) | copy-start | bytes 393220
  265.8 621.6 %copy-start.3 = (f32[256,1536]{1,0:T(8,128)}, f32[256,1536]{1,0:T(8,128)S(1)}, u32[]{:S(2)}) copy-start(f32[256,1536]{1,0:T(8,128)S(1)} %get-tuple-element.93) | copy-start | bytes 4718596
  611.1 77.1 %all-to-all-start.1 = ((bf16[4,5,104,1536]{3,2,1,0:T(8,128)(2,1)}), bf16[4,5,104,1536]{3,2,1,0:T(8,128)(2,1)}, u32[]{:S(2)}, u32[]{:S(2)}) async-start(bf16[4,5,104,1536]{3,2,1,0:T(8,128)(2,1)} %copy.89), calls=%async_computation.1 | async-start | bytes 12779520 | tf_op jit(solution)/shard_map/all_to_all | solution.py:161
  693.5 194.0 %copy-start.21 = (bf16[256,20]{0,1:T(8,128)(2,1)}, bf16[256,20]{0,1:T(8,128)(2,1)S(1)}, u32[]{:S(2)}) copy-start(bf16[256,20]{0,1:T(8,128)(2,1)S(1)} %get-tuple-element.59) | copy-start | bytes 30724
  805.6 77.0 %all-to-all-start.3 = ((bf16[4,5,104,1536]{3,2,1,0:T(8,128)(2,1)}), bf16[4,5,104,1536]{3,2,1,0:T(8,128)(2,1)}, u32[]{:S(2)}, u32[]{:S(2)}) async-start(bf16[4,5,104,1536]{3,2,1,0:T(8,128)(2,1)} %copy.91), calls=%async_computation.3 | async-start | bytes 12779520 | tf_op jit(solution)/shard_map/all_to_all | solution.py:203
  810.9 155.8 %reduce-scatter.18.cloned.1.call-start = ((), (), s32[]{:S(2)}) async-start(), calls=%async_computation.19 | async-start | bytes 1769472 | tf_op jit(solution)/shard_map/reduce_scatter | solution.py:267
  903.7 131.2 %reduce-scatter.16.cloned.1.call-start = ((), (), s32[]{:S(2)}) async-start(), calls=%async_computation.18 | async-start | bytes 1769472 | tf_op jit(solution)/shard_map/reduce_scatter | solution.py:264
  917.2 216.0 %reduce-scatter.20.cloned.1.call-start = ((), (), s32[]{:S(2)}) async-start(), calls=%async_computation.20 | async-start | bytes 5308416 | tf_op jit(solution)/shard_map/reduce_scatter | solution.py:270
  922.0 310.1 %reduce-scatter.14.cloned.1.call-start = ((), (), s32[]{:S(2)}) async-start(), calls=%async_computation.17 | async-start | bytes 5308416 | tf_op jit(solution)/shard_map/reduce_scatter | solution.py:261
  929.9 367.9 %reduce-scatter.22.cloned.1.call-start = ((), (), s32[]{:S(2)}) async-start(), calls=%async_computation.21 | async-start | bytes 442368
  931.8 410.6 %all-reduce.10.cloned.1.call-start = ((), (), s32[]{:S(2)}) async-start(), calls=%async_computation.24 | async-start | bytes 3145728 | tf_op jit(solution)/shard_map/psum | solution.py:282
  1232.1 254.1 %reduce-scatter.26.cloned.1.call-start = ((), (), s32[]{:S(2)}) async-start(), calls=%async_computation.23 | async-start | bytes 8847360
  1253.6 486.4 %reduce-scatter.24.cloned.1.call-start = ((), (), s32[]{:S(2)}) async-start(), calls=%async_computation.22 | async-start | bytes 17694720
  (33 other events, 294.0 us)
Sparse Core Ops, SparseCore 0:
  10.2 47.3 all-gather.7
  59.7 42.5 all-gather.9
  104.5 77.6 all-gather.11
  184.2 77.6 all-gather.13
  264.0 212.8 all-gather.15
  478.9 116.1 all-gather.17
  903.8 62.8 reduce-scatter.17
  970.7 64.1 reduce-scatter.15
  1038.6 94.6 reduce-scatter.19
  1136.7 95.3 reduce-scatter.13
  1235.9 61.8 reduce-scatter.21
  1300.2 42.1 all-reduce.9
  1346.1 140.1 reduce-scatter.25
  1489.7 250.3 reduce-scatter.23
where the time goes:
time: 1760 us; the launch traced here: 1750 us
  waiting for transfers between devices  1250 us (71%)
  blocking collectives  237 us (13%)
  matrix products  149 us (8%)
  local copies, waits for them, and re-layouts  66.5 us (4%)
  other arithmetic  23.9 us (1%)
    unnamed x17, waiting for transfers between devices  392 us
    dot_general x33, matrix products, product(): return jnp.einsum(form, left, right, preferred_element_type=jnp.float32)  149 us
    all_gather x1, waiting for transfers between devices, on_device(): lax.all_gather(gate_up_weight, 'shard', axis=0, tiled=True)  133 us
    all_gather x1, waiting for transfers between devices, on_device(): lax.all_gather(down_weight, 'shard', axis=0, tiled=True)  99.9 us
    reduce_scatter x1, waiting for transfers between devices, on_device(): lax.psum_scatter(query_term.astype(jnp.bfloat16), 'shard', scatter_dimens...  98.8 us
    reduce_scatter x1, waiting for transfers between devices, on_device(): lax.psum_scatter(output_term.astype(jnp.bfloat16), 'shard', scatter_dimen...  98.3 us
    all_gather x1, waiting for transfers between devices, on_device(): lax.all_gather(query_weight, 'shard', axis=0, tiled=True)  77.6 us
    all_to_all x1, blocking collectives, on_device(): lax.all_to_all(grad_rows, 'expert', split_axis=0, concat_axis=0, tiled=True)  75.7 us
  transfers between devices with their start and end apart: 16, of which 15 were waited for; matrix products, arithmetic and copies ran while one was open for 8% of the time, Pallas kernels for 0%

commit v1 on v0

--- a/solution.py
+++ b/solution.py
@@ -5,6 +5,27 @@
 
 HEAD_DIM = 64
 norm_eps = 1e-06
+
+
+def paths_order(shard_in):
+    extra = jax.lax.axis_index("shard")
+    item_now = jax.lax.axis_size("shard")
+    mid_arr, taken_in, n_now = (item_now, extra, shard_in.shape[0])
+    piece_now, s_next = (shard_in, 1)
+    while s_next < mid_arr:
+        piece_now = jnp.concatenate(
+            [
+                piece_now,
+                jax.lax.ppermute(
+                    piece_now,
+                    axis_name="shard",
+                    perm=[(k0, (k0 - s_next) % mid_arr) for k0 in range(mid_arr)],
+                ),
+            ],
+            axis=0,
+        )
+        s_next = 2 * s_next
+    return jnp.roll(piece_now, shift=taken_in * n_now, axis=0)
 
 
 def product(form, left, right):
@@ -92,7 +113,7 @@
     )
     gate_up_full, down_full = (
         lax.all_gather(gate_up_weight, "shard", axis=0, tiled=True),
-        lax.all_gather(down_weight, "shard", axis=0, tiled=True),
+        paths_order(down_weight),
     )
     gain_one = gain_one.astype(jnp.float32)
     gain_two = gain_two.astype(jnp.float32)

time: 1760 us -> 1880 us (1.068)
  waiting for transfers between devices: 1250 us -> 1450 us
  blocking collectives: 237 us -> 105 us
    ppermute x0 -> x3, waiting for transfers between devices: none -> 333 us  [paths_order(): jax.lax.ppermute(piece_now, axis_name='shard', perm=[(k0, (k0 - s_next) %...]
    all_to_all x2 -> x0, blocking collectives: 151 us -> none  [the longest x1 75.7 us: on_device(): lax.all_to_all(grad_rows, 'expert', split_axis=0, concat_axis=0, tiled=True)]
    all_gather x1, waiting for transfers between devices: 133 us -> 0.49 us  [on_device(): lax.all_gather(gate_up_weight, 'shard', axis=0, tiled=True)]
    all_gather x1, waiting for transfers between devices: 99.9 us -> 0.02 us  [on_device(): lax.all_gather(down_weight, 'shard', axis=0, tiled=True)]
    all_to_all x0 -> x2, waiting for transfers between devices: none -> 71.7 us  [the longest x1 71.7 us: on_device(): lax.all_to_all(grad_rows, 'expert', split_axis=0, concat_axis=0, tiled=True)]
    all_gather x1, waiting for transfers between devices: 42.6 us -> 80.9 us  [on_device(): lax.all_gather(key_matrix, 'shard', axis=0, tiled=True)]
    unnamed x98 -> x155, local copies, waits for them, and re-layouts: 52 us -> 66.1 us
  transfers between devices with their start and end apart: 16 -> 21, of which waited for: 15 -> 16; matrix products, arithmetic and copies ran while one was open for 8% -> 11% of each run, Pallas kernels for 0% -> 0%
where the time goes in v1:
time: 1880 us; the launch traced here: 1870 us
  waiting for transfers between devices  1450 us (77%)
  matrix products  154 us (8%)
  blocking collectives  105 us (6%)
  local copies, waits for them, and re-layouts  85 us (5%)
  starting transfers between devices  30.5 us (2%)
  other arithmetic  26.1 us (1%)
    unnamed x17, waiting for transfers between devices  395 us
    ppermute x3, waiting for transfers between devices, paths_order(): jax.lax.ppermute(piece_now, axis_name='shard', perm=[(k0, (k0 - s_next) %...  333 us
    dot_general x33, matrix products, product(): return jnp.einsum(form, left, right, preferred_element_type=jnp.float32)  154 us
    reduce_scatter x1, waiting for transfers between devices, on_device(): lax.psum_scatter(output_term.astype(jnp.bfloat16), 'shard', scatter_dimen...  98.8 us
    reduce_scatter x1, waiting for transfers between devices, on_device(): lax.psum_scatter(query_term.astype(jnp.bfloat16), 'shard', scatter_dimens...  98.1 us
    all_gather x1, waiting for transfers between devices, on_device(): lax.all_gather(key_matrix, 'shard', axis=0, tiled=True)  80.9 us
    all_gather x1, waiting for transfers between devices, on_device(): lax.all_gather(query_weight, 'shard', axis=0, tiled=True)  77.6 us
    all_to_all x1, waiting for transfers between devices, on_device(): lax.all_to_all(grad_rows, 'expert', split_axis=0, concat_axis=0, tiled=True)  71.7 us
  transfers between devices with their start and end apart: 21, of which 16 were waited for; matrix products, arithmetic and copies ran while one was open for 11% of the time, Pallas kernels for 0%

profile of v1, /device:TPU:0, one launch (start us, length us, event | category | flops | bytes accessed | tf_op | source)
XLA Modules:
  0.0 1865.8 jit_solution(6028106457925464057)
XLA Ops:
  18.5 41.1 %all-reduce.5 = (bf16[1536]{0:T(1024)(128)(2,1)S(1)}, bf16[1536]{0:T(1024)(128)(2,1)S(1)}) all-reduce(bf16[1536]{0:T(1024)(128)(2,1)S(1)} %dynamic-update-slice, bf16[1536]{0:T(1024)(128)(2,1)S(1)} %dynamic-update-slice.1), channel_id=1, replica_groups=mesh['expert'=4,'shard'=8] {'shard'}, use_global_device_ids=true, to_apply=%add | all-reduce | flops 3072 | bytes 12288
  73.7 80.9 %all-gather.10.cloned.1.call-done = bf16[1536,512]{1,0:T(8,128)(2,1)} async-done(((bf16[192,512]{1,0:T(8,128)(2,1)}), bf16[1536,512]{1,0:T(8,128)(2,1)}) %all-gather.10.cloned.1.call-update) | async-done | bytes 1572880 | tf_op jit(solution)/shard_map/all_gather | solution.py:108
  156.9 77.6 %all-gather.12.cloned.1.call-done = bf16[1536,1536]{1,0:T(8,128)(2,1)} async-done(((bf16[192,1536]{1,0:T(8,128)(2,1)}), bf16[1536,1536]{1,0:T(8,128)(2,1)}) %all-gather.12.cloned.1.call-update) | async-done | bytes 4718608 | tf_op jit(solution)/shard_map/all_gather | solution.py:107
  244.2 70.0 %all-gather.14.cloned.1.call-done = bf16[1536,1536]{1,0:T(8,128)(2,1)} async-done(((bf16[192,1536]{1,0:T(8,128)(2,1)}), bf16[1536,1536]{1,0:T(8,128)(2,1)}) %all-gather.14.cloned.1.call-update) | async-done | bytes 4718608 | tf_op jit(solution)/shard_map/all_gather | solution.py:110
  340.6 332.8 %collective-permute-done.2 = bf16[768,5,512]{2,0,1:T(8,128)(2,1)} collective-permute-done((bf16[768,5,512]{2,0,1:T(8,128)(2,1)}, bf16[768,5,512]{2,0,1:T(8,128)(2,1)}, u32[]{:S(2)}, u32[]{:S(2)}) %collective-permute-start.2) | collective-permute-done | bytes 3932192 | tf_op jit(solution)/shard_map/ppermute | solution.py:19
  688.0 12.1 fusion.27
  727.8 32.1 %all-gather = bf16[8,192,20]{1,2,0:T(8,128)(2,1)S(1)} all-gather(bf16[1,192,20]{1,2,0:T(8,128)(2,1)S(1)} %bitcast.205), channel_id=1, replica_groups=mesh['expert'=4,'shard'=8] {'shard'}, dimensions={0}, use_global_device_ids=true | all-gather | bytes 69120 | tf_op jit(solution)/shard_map/all_gather | solution.py:112
  760.3 39.1 %all-to-all-done.1 = bf16[4,5,104,1536]{3,2,1,0:T(8,128)(2,1)} async-done(((bf16[4,5,104,1536]{3,2,1,0:T(8,128)(2,1)}), bf16[4,5,104,1536]{3,2,1,0:T(8,128)(2,1)}, u32[]{:S(2)}, u32[]{:S(2)}) %all-to-all-start.1) | async-done | bytes 6389792 | tf_op jit(solution)/shard_map/all_to_all | solution.py:182
  814.6 71.7 %all-to-all-done.2 = bf16[4,5,104,1536]{3,2,1,0:T(8,128)(2,1)} async-done(((bf16[4,5,104,1536]{3,2,1,0:T(8,128)(2,1)}), bf16[4,5,104,1536]{3,2,1,0:T(8,128)(2,1)}, u32[]{:S(2)}, u32[]{:S(2)}) %all-to-all-start.2) | async-done | bytes 6389792 | tf_op jit(solution)/shard_map/all_to_all | solution.py:196
  886.3 14.0 fusion.24
  900.3 13.3 convert_bitcast_fusion
  925.4 71.4 %all-to-all-done.3 = bf16[4,5,104,1536]{3,2,1,0:T(8,128)(2,1)} async-done(((bf16[4,5,104,1536]{3,2,1,0:T(8,128)(2,1)}), bf16[4,5,104,1536]{3,2,1,0:T(8,128)(2,1)}, u32[]{:S(2)}, u32[]{:S(2)}) %all-to-all-start.3) | async-done | bytes 6389792 | tf_op jit(solution)/shard_map/all_to_all | solution.py:224
  1044.1 35.8 %reduce-scatter.18.cloned.1.call-done = bf16[192,512]{1,0:T(8,128)(2,1)} async-done(((bf16[1536,512]{1,0:T(8,128)(2,1)}), bf16[192,512]{1,0:T(8,128)(2,1)}) %reduce-scatter.18.cloned.1.call-update) | async-done | bytes 196624 | tf_op jit(solution)/shard_map/reduce_scatter | solution.py:288
  1079.9 68.3 %reduce-scatter.16.cloned.1.call-done = bf16[192,512]{1,0:T(8,128)(2,1)} async-done(((bf16[1536,512]{1,0:T(8,128)(2,1)}), bf16[192,512]{1,0:T(8,128)(2,1)}) %reduce-scatter.16.cloned.1.call-update) | async-done | bytes 196624 | tf_op jit(solution)/shard_map/reduce_scatter | solution.py:285
  1148.3 98.1 %reduce-scatter.14.cloned.1.call-done = bf16[192,1536]{1,0:T(8,128)(2,1)} async-done(((bf16[1536,1536]{1,0:T(8,128)(2,1)}), bf16[192,1536]{1,0:T(8,128)(2,1)}) %reduce-scatter.14.cloned.1.call-update) | async-done | bytes 589840 | tf_op jit(solution)/shard_map/reduce_scatter | solution.py:282
  1246.4 98.8 %reduce-scatter.20.cloned.1.call-done = bf16[192,1536]{1,0:T(8,128)(2,1)} async-done(((bf16[1536,1536]{1,0:T(8,128)(2,1)}), bf16[192,1536]{1,0:T(8,128)(2,1)}) %reduce-scatter.20.cloned.1.call-update) | async-done | bytes 589840 | tf_op jit(solution)/shard_map/reduce_scatter | solution.py:291
  1345.3 10.8 bitcast_convert_fusion.1
  1356.1 10.4 copy.127
  1366.6 15.2 bitcast_convert_fusion
  1381.8 19.6 %copy.125 = bf16[1536,5120]{1,0:T(8,128)(2,1)} copy(bf16[1536,5120]{0,1:T(8,128)(2,1)} %bitcast.178) | data formatting | bytes 31457280
  1419.3 19.7 %all-reduce.4 = (bf16[1536]{0:T(1024)(128)(2,1)S(1)}, bf16[1536]{0:T(1024)(128)(2,1)S(1)}) all-reduce(bf16[1536]{0:T(1024)(128)(2,1)S(1)} %get-tuple-element.57, bf16[1536]{0:T(1024)(128)(2,1)S(1)} %copy-done.57), channel_id=2, replica_groups=mesh['expert'=4,'shard'=8] {'shard'}, use_global_device_ids=true, to_apply=%region_16.17.clone | all-reduce | flops 3072 | bytes 12288
  1439.2 11.7 all-reduce.6
  1460.7 138.7 %reduce-scatter.26.cloned.1.call-done = bf16[192,2560]{1,0:T(8,128)(2,1)} async-done(((bf16[1536,2560]{1,0:T(8,128)(2,1)}), bf16[192,2560]{1,0:T(8,128)(2,1)}) %reduce-scatter.26.cloned.1.call-update) | async-done | bytes 983056
  1602.5 250.7 %reduce-scatter.24.cloned.1.call-done = bf16[192,5120]{1,0:T(8,128)(2,1)} async-done(((bf16[1536,5120]{1,0:T(8,128)(2,1)}), bf16[192,5120]{1,0:T(8,128)(2,1)}) %reduce-scatter.24.cloned.1.call-update) | async-done | bytes 1966096
  (272 shorter events, 214.4 us)
Async XLA Ops:
  7.2 64.3 %all-gather.8.cloned.1.call-start = ((), (), s32[]{:S(2)}) async-start(), calls=%async_computation.11 | async-start | bytes 1769472 | tf_op jit(solution)/shard_map/all_gather | solution.py:109
  8.0 146.6 %all-gather.10.cloned.1.call-start = ((), (), s32[]{:S(2)}) async-start(), calls=%async_computation.12 | async-start | bytes 1769472 | tf_op jit(solution)/shard_map/all_gather | solution.py:108
  8.7 225.8 %all-gather.12.cloned.1.call-start = ((), (), s32[]{:S(2)}) async-start(), calls=%async_computation.13 | async-start | bytes 5308416 | tf_op jit(solution)/shard_map/all_gather | solution.py:107
  9.5 304.8 %all-gather.14.cloned.1.call-start = ((), (), s32[]{:S(2)}) async-start(), calls=%async_computation.14 | async-start | bytes 5308416 | tf_op jit(solution)/shard_map/all_gather | solution.py:110
  10.0 678.0 %all-gather.16.cloned.1.call-start = ((), (), s32[]{:S(2)}) async-start(), calls=%async_computation.15 | async-start | bytes 17694720 | tf_op jit(solution)/shard_map/all_gather | solution.py:115
  10.6 51.8 %collective-permute-start = (bf16[192,5,512]{2,0,1:T(8,128)(2,1)S(1)}, bf16[192,5,512]{2,0,1:T(8,128)(2,1)S(1)}, u32[]{:S(2)}, u32[]{:S(2)}) collective-permute-start(bf16[192,5,512]{2,0,1:T(8,128)(2,1)S(1)} %copy-done.3), channel_id=1, source_target_pairs={{0,7},{1,0},{2,1},{3,2},{4,3},{5,4},{6,5},{7,6},{8,15},{9,8},{10,9... | collective-permute-start | bytes 2949128 | tf_op jit(solution)/shard_map/ppermute | solution.py:19
  62.3 176.6 %copy-start.23 = (f32[256,32]{0,1:T(8,128)}, f32[256,32]{0,1:T(8,128)S(1)}, u32[]{:S(2)}) copy-start(f32[256,32]{0,1:T(8,128)S(1)} %get-tuple-element.88) | copy-start | bytes 98308
  62.3 176.6 %copy-start.26 = (f32[256,32]{0,1:T(8,128)}, f32[256,32]{0,1:T(8,128)S(1)}, u32[]{:S(2)}) copy-start(f32[256,32]{0,1:T(8,128)S(1)} %get-tuple-element.89) | copy-start | bytes 98308
  63.9 266.2 %collective-permute-start.1 = (bf16[384,5,512]{2,0,1:T(8,128)(2,1)}, bf16[384,5,512]{2,0,1:T(8,128)(2,1)}, u32[]{:S(2)}, u32[]{:S(2)}) collective-permute-start(bf16[384,5,512]{2,0,1:T(8,128)(2,1)} %pad_maximum_fusion.4), channel_id=1, source_target_pairs={{0,6},{1,7},{2,0},{3,1},{4,2},{5,3},{6,4},{7,5},{8,14},{9,15},{10,... | collective-permute-start | bytes 5898248 | tf_op jit(solution)/shard_map/ppermute | solution.py:19
  324.5 363.0 %all-to-all-start = ((bf16[4,5,104,1536]{3,2,1,0:T(8,128)(2,1)}), bf16[4,5,104,1536]{3,2,1,0:T(8,128)(2,1)}, u32[]{:S(2)}, u32[]{:S(2)}) async-start(bf16[4,5,104,1536]{3,2,1,0:T(8,128)(2,1)} %bitcast.177), calls=%async_computation | async-start | bytes 12779520 | tf_op jit(solution)/shard_map/all_to_all | solution.py:176
  329.9 484.7 %all-gather.18.cloned.1.call-start = ((), (), s32[]{:S(2)}) async-start(), calls=%async_computation.16 | async-start | bytes 8847360 | tf_op jit(solution)/shard_map/all_gather | solution.py:206
  333.5 339.8 %collective-permute-start.2 = (bf16[768,5,512]{2,0,1:T(8,128)(2,1)}, bf16[768,5,512]{2,0,1:T(8,128)(2,1)}, u32[]{:S(2)}, u32[]{:S(2)}) collective-permute-start(bf16[768,5,512]{2,0,1:T(8,128)(2,1)} %pad_maximum_fusion.1), channel_id=1, source_target_pairs={{0,4},{1,5},{2,6},{3,7},{4,0},{5,1},{6,2},{7,3},{8,12},{9,13},{10,... | collective-permute-start | bytes 11796488 | tf_op jit(solution)/shard_map/ppermute | solution.py:19
  722.4 77.1 %all-to-all-start.1 = ((bf16[4,5,104,1536]{3,2,1,0:T(8,128)(2,1)}), bf16[4,5,104,1536]{3,2,1,0:T(8,128)(2,1)}, u32[]{:S(2)}, u32[]{:S(2)}) async-start(bf16[4,5,104,1536]{3,2,1,0:T(8,128)(2,1)} %copy.89), calls=%async_computation.1 | async-start | bytes 12779520 | tf_op jit(solution)/shard_map/all_to_all | solution.py:182
  804.6 197.1 %copy-start.43 = (bf16[256,20]{0,1:T(8,128)(2,1)}, bf16[256,20]{0,1:T(8,128)(2,1)S(1)}, u32[]{:S(2)}) copy-start(bf16[256,20]{0,1:T(8,128)(2,1)S(1)} %get-tuple-element.59) | copy-start | bytes 30724
  809.3 77.0 %all-to-all-start.2 = ((bf16[4,5,104,1536]{3,2,1,0:T(8,128)(2,1)}), bf16[4,5,104,1536]{3,2,1,0:T(8,128)(2,1)}, u32[]{:S(2)}, u32[]{:S(2)}) async-start(bf16[4,5,104,1536]{3,2,1,0:T(8,128)(2,1)} %bitcast.183), calls=%async_computation.2 | async-start | bytes 12779520 | tf_op jit(solution)/shard_map/all_to_all | solution.py:196
  919.6 77.2 %all-to-all-start.3 = ((bf16[4,5,104,1536]{3,2,1,0:T(8,128)(2,1)}), bf16[4,5,104,1536]{3,2,1,0:T(8,128)(2,1)}, u32[]{:S(2)}, u32[]{:S(2)}) async-start(bf16[4,5,104,1536]{3,2,1,0:T(8,128)(2,1)} %copy.91), calls=%async_computation.3 | async-start | bytes 12779520 | tf_op jit(solution)/shard_map/all_to_all | solution.py:224
  925.1 154.9 %reduce-scatter.18.cloned.1.call-start = ((), (), s32[]{:S(2)}) async-start(), calls=%async_computation.19 | async-start | bytes 1769472 | tf_op jit(solution)/shard_map/reduce_scatter | solution.py:288
  1016.6 131.7 %reduce-scatter.16.cloned.1.call-start = ((), (), s32[]{:S(2)}) async-start(), calls=%async_computation.18 | async-start | bytes 1769472 | tf_op jit(solution)/shard_map/reduce_scatter | solution.py:285
  1029.4 217.0 %reduce-scatter.14.cloned.1.call-start = ((), (), s32[]{:S(2)}) async-start(), calls=%async_computation.17 | async-start | bytes 5308416 | tf_op jit(solution)/shard_map/reduce_scatter | solution.py:282
  1037.2 308.1 %reduce-scatter.20.cloned.1.call-start = ((), (), s32[]{:S(2)}) async-start(), calls=%async_computation.20 | async-start | bytes 5308416 | tf_op jit(solution)/shard_map/reduce_scatter | solution.py:291
  1042.2 368.8 %reduce-scatter.22.cloned.1.call-start = ((), (), s32[]{:S(2)}) async-start(), calls=%async_computation.21 | async-start | bytes 442368
  1044.1 411.6 %all-reduce.10.cloned.1.call-start = ((), (), s32[]{:S(2)}) async-start(), calls=%async_computation.24 | async-start | bytes 3145728 | tf_op jit(solution)/shard_map/psum | solution.py:303
  1345.3 254.1 %reduce-scatter.26.cloned.1.call-start = ((), (), s32[]{:S(2)}) async-start(), calls=%async_computation.23 | async-start | bytes 8847360
  1366.6 486.7 %reduce-scatter.24.cloned.1.call-start = ((), (), s32[]{:S(2)}) async-start(), calls=%async_computation.22 | async-start | bytes 17694720
  (63 other events, 1278.5 us)
Sparse Core Ops, SparseCore 0:
  10.2 61.2 all-gather.7
  73.7 80.8 all-gather.9
  156.8 77.6 all-gather.11
  236.5 77.6 all-gather.13
  316.3 371.6 all-gather.15
  690.1 117.3 all-gather.17
  1016.7 63.1 reduce-scatter.17
  1083.9 64.2 reduce-scatter.15
  1151.9 94.4 reduce-scatter.13
  1249.9 95.3 reduce-scatter.19
  1349.1 61.8 reduce-scatter.21
  1413.4 42.1 all-reduce.9
  1459.2 140.1 reduce-scatter.25
  1602.8 250.3 reduce-scatter.23
